TPU v7x, 768 devices: a whole 4x8x12 slice. The times are simulated.
768 devices in a mesh: batch: 8 (over x, core), ctx: 48 (over z, y_hi), head: 2 (over y_lo).
Axes of the slice: x: 4, y: 8 (y_hi: 4, y_lo: 2; y = y_hi * 2 + y_lo), z: 12, core: 2. Of those that a mesh axis runs over, the one named last changes fastest.
Arguments:
- queries: bfloat16 [2, 49152, 1536], P(None, ('batch', 'ctx'), 'head'), parts along dimension 1, may hold values from -6 to 6
- keyvals: bfloat16 [4, 49152, 1536], P(None, ('batch', 'ctx'), 'head'), parts along dimension 1, may hold values from -6 to 6
- w_out: bfloat16 [1536, 3072], P('head'), may hold values from -2.390625 to 2.390625
Outputs:
- output: bfloat16 [49152, 3072], P(('batch', 'ctx'), 'head'), parts along dimension 0
- output_tangent: bfloat16 [49152, 3072], P(('batch', 'ctx'), 'head'), parts along dimension 0
There are 8 independent parts, one for each index of `batch`. A program takes and returns all parts, laid end to end along the dimension named above; an argument that names none is the same for every part. Nothing has to cross between parts.
All inputs are finite; a program needn't handle non-finite values.
Results may differ from a plain program's by a relative error of at most 0.01.
Values may be sent and summed in bfloat16 or wider, within the bound.
No kernel may reach another device: no remote copies, remote signals or barrier semaphores. Data moves between devices by JAX's collectives and lax.ppermute only.
A program may use at most 32 MiB of HBM per device.

v0:
```python
import math

import jax
import jax.numpy as jnp
from jax import lax
from jax.sharding import PartitionSpec as P

HD = 128
RADIUS = 2


def from_behind(shard, axis, by):
    peers = lax.axis_size(axis)
    pairs = [(i, i + by) for i in range(peers) if 0 <= i + by < peers]
    return lax.ppermute(shard, axis, pairs)


def attend(query_pair, key_block, visible, w_out):
    row_count = query_pair.shape[1]
    key_count = key_block.shape[1]
    head_count = query_pair.shape[2] // HD
    score_scale = 1.0 / math.sqrt(HD)
    query_now = query_pair[0].reshape(row_count, head_count, HD)
    query_tan = query_pair[1].reshape(row_count, head_count, HD)
    key_now = key_block[0].reshape(key_count, head_count, HD)
    value_now = key_block[1].reshape(key_count, head_count, HD)
    key_tan = key_block[2].reshape(key_count, head_count, HD)
    value_tan = key_block[3].reshape(key_count, head_count, HD)
    scores = (
        jnp.einsum("qhd,khd->hqk", query_now, key_now, preferred_element_type=jnp.float32)
        * score_scale
    )
    scores = jnp.where(visible[None, None, :], scores, -jnp.inf)
    row_max = jnp.max(scores, axis=-1, keepdims=True)
    expo = jnp.exp(scores - row_max)
    prob_f = expo / jnp.sum(expo, axis=-1, keepdims=True)
    query_joined = jnp.concatenate([query_tan, query_now], axis=2)
    key_joined = jnp.concatenate([key_now, key_tan], axis=2)
    tan_scores = (
        jnp.einsum("qhd,khd->hqk", query_joined, key_joined, preferred_element_type=jnp.float32)
        * score_scale
    )
    weighted = prob_f * tan_scores
    tan_shift = jnp.sum(weighted, axis=-1)
    prob_b = prob_f.astype(jnp.bfloat16)
    weight_b = weighted.astype(jnp.bfloat16)
    attended = jnp.einsum("hqk,khd->qhd", prob_b, value_now, preferred_element_type=jnp.float32)
    att_tan = (
        jnp.einsum("hqk,khd->qhd", weight_b, value_now, preferred_element_type=jnp.float32)
        + jnp.einsum("hqk,khd->qhd", prob_b, value_tan, preferred_element_type=jnp.float32)
        - jnp.transpose(tan_shift)[:, :, None] * attended
    )
    att_flat = attended.reshape(row_count, head_count * HD).astype(jnp.bfloat16)
    tan_flat = att_tan.reshape(row_count, head_count * HD).astype(jnp.bfloat16)
    projected = jnp.dot(att_flat, w_out, preferred_element_type=jnp.float32)
    projected_tan = jnp.dot(tan_flat, w_out, preferred_element_type=jnp.float32)
    return (projected, projected_tan)


def per_device(queries, keyvals, w_out):
    row_count = queries.shape[1]
    ctx_count = lax.axis_size("ctx")
    ctx_place = lax.axis_index("ctx")
    behind = []
    ahead = []
    going_up = keyvals
    going_down = keyvals
    for stride in range(RADIUS):
        going_up = from_behind(going_up, "ctx", 1)
        going_down = from_behind(going_down, "ctx", -1)
        behind.append(going_up)
        ahead.append(going_down)
    ordered = behind[::-1] + [keyvals] + ahead
    key_block = jnp.concatenate(ordered, axis=1)
    key_count = key_block.shape[1]
    offsets = jnp.arange(key_count, dtype=jnp.int32) // row_count - RADIUS
    target = ctx_place + offsets
    visible = (target >= 0) & (target < ctx_count)
    projected, projected_tan = attend(queries, key_block, visible, w_out)
    summed = (
        lax.psum_scatter(projected, "head", scatter_dimension=1, tiled=True),
        lax.psum_scatter(projected_tan, "head", scatter_dimension=1, tiled=True),
    )
    return (summed[0].astype(jnp.bfloat16), summed[1].astype(jnp.bfloat16))


def solution(mesh):
    in_specs = (
        P(None, ("batch", "ctx"), "head"),
        P(None, ("batch", "ctx"), "head"),
        P("head", None),
    )
    out_specs = (P(("batch", "ctx"), "head"), P(("batch", "ctx"), "head"))
    return jax.shard_map(
        per_device, mesh=mesh, in_specs=in_specs, out_specs=out_specs, check_vma=False
    )
```

profile of v0, /device:TPU:1, one launch (start us, length us, event | category | flops | bytes accessed | tf_op | source)
XLA Modules:
  0.0 200.9 jit_solution(12650240328285248353)
XLA Ops:
  7.2 1.5 copy.11
  8.7 5.1 %collective-permute-start = (bf16[4,128,768]{1,2,0:T(8,128)(2,1)S(1)}, bf16[4,128,768]{1,2,0:T(8,128)(2,1)S(1)}, u32[]{:S(2)}, u32[]{:S(2)}) collective-permute-start(bf16[4,128,768]{1,2,0:T(8,128)(2,1)S(1)} %copy.11), channel_id=1, source_target_pairs={{0,2},{2,4},{4,6},{6,8},{8,10},{10,12},{12,14},{14,16},{16,18},{18... | collective-permute-start | bytes 2359304 | tf_op jit(solution)/shard_map/ppermute | solution.py:15
  13.8 1.3 collective-permute-start.2
  15.1 9.2 %collective-permute-done = bf16[4,128,768]{1,2,0:T(8,128)(2,1)S(1)} collective-permute-done((bf16[4,128,768]{1,2,0:T(8,128)(2,1)S(1)}, bf16[4,128,768]{1,2,0:T(8,128)(2,1)S(1)}, u32[]{:S(2)}, u32[]{:S(2)}) %collective-permute-start) | collective-permute-done | bytes 786464 | tf_op jit(solution)/shard_map/ppermute | solution.py:15
  24.3 12.0 %collective-permute-start.1 = (bf16[4,128,768]{1,2,0:T(8,128)(2,1)S(1)}, bf16[4,128,768]{1,2,0:T(8,128)(2,1)}, u32[]{:S(2)}, u32[]{:S(2)}) collective-permute-start(bf16[4,128,768]{1,2,0:T(8,128)(2,1)S(1)} %collective-permute-done), channel_id=1, source_target_pairs={{0,2},{2,4},{4,6},{6,8},{8,10},{10,12},{12,14},{14,16},{16,18},{18... | collective-permute-start | bytes 2359304 | tf_op jit(solution)/shard_map/ppermute | solution.py:15
  36.3 20.2 %collective-permute-done.2 = bf16[4,128,768]{1,2,0:T(8,128)(2,1)S(1)} collective-permute-done((bf16[4,128,768]{1,2,0:T(8,128)(2,1)S(1)}, bf16[4,128,768]{1,2,0:T(8,128)(2,1)S(1)}, u32[]{:S(2)}, u32[]{:S(2)}) %collective-permute-start.2) | collective-permute-done | bytes 786464 | tf_op jit(solution)/shard_map/ppermute | solution.py:15
  56.4 1.3 collective-permute-start.3
  57.7 1.7 fusion.36
  59.6 0.8 copy.20
  60.4 1.1 copy.33
  61.5 0.8 copy.19
  62.4 1.3 constant_dynamic-update-slice_fusion.4
  64.2 34.3 %collective-permute-done.3 = bf16[4,128,768]{1,2,0:T(8,128)(2,1)S(1)} collective-permute-done((bf16[4,128,768]{1,2,0:T(8,128)(2,1)S(1)}, bf16[4,128,768]{1,2,0:T(8,128)(2,1)S(1)}, u32[]{:S(2)}, u32[]{:S(2)}) %collective-permute-start.3) | collective-permute-done | bytes 786464 | tf_op jit(solution)/shard_map/ppermute | solution.py:15
  98.7 1.3 fusion.35
  100.0 2.2 %copy.21 = bf16[640,6,128]{2,0,1:T(8,128)(2,1)} copy(bf16[640,6,128]{0,2,1:T(8,128)(2,1)} %bitcast.48) | data formatting | bytes 1966080 | tf_op jit(solution)/shard_map/reshape;squeeze | solution.py:25
  102.3 3.4 %fusion.37 = (f32[6,128]{1,0:T(8,128)S(1)}, f32[6,128,640]{1,2,0:T(8,128)}) fusion(pred[640]{0:T(1024)(128)(4,1)S(1)} %fusion.30, bf16[640,6,128]{0,2,1:T(8,128)(2,1)} %bitcast.49, bf16[128,6,128]{0,2,1:T(8,128)(2,1)S(1)} %bitcast.53), kind=kOutput, calls=%fused_computation.48 | convolution fusion | flops 127795840 | bytes 3149440 | tf_op jit(solution)/shard_map/sub | solution.py:35
  105.6 1.3 copy.22
  106.9 1.7 fusion.18
  112.3 2.0 fusion.42
  114.4 4.3 %fusion.40 = f32[128,3072]{1,0:T(8,128)} fusion(bf16[128,768]{0,1:T(8,128)(2,1)S(1)} %bitcast.50, bf16[768,3072]{1,0:T(8,128)(2,1)} %param.5), kind=kOutput, calls=%fused_computation.51 | convolution fusion | flops 603979776 | bytes 6488064 | tf_op jit(solution)/shard_map/dot_general | solution.py:55
  118.7 33.1 %reduce-scatter.5.cloned.1.call-done = f32[128,1536]{1,0:T(8,128)} async-done(((f32[128,3072]{1,0:T(8,128)}), f32[128,1536]{1,0:T(8,128)}) %reduce-scatter.5.cloned.1.call-update) | async-done | bytes 786448 | tf_op jit(solution)/shard_map/reduce_scatter | solution.py:82
  151.8 1.9 convert_element_type.31
  153.8 38.4 %reduce-scatter.3.cloned.1.call-done = f32[128,1536]{1,0:T(8,128)} async-done(((f32[128,3072]{1,0:T(8,128)}), f32[128,1536]{1,0:T(8,128)}) %reduce-scatter.3.cloned.1.call-update) | async-done | bytes 786448 | tf_op jit(solution)/shard_map/reduce_scatter | solution.py:81
  192.2 1.9 convert_element_type.27
  (30 shorter events, 4.6 us)
Async XLA Ops:
  7.2 144.7 %reduce-scatter.5.cloned.1.call-start = ((), (), s32[]{:S(2)}) async-start(), calls=%async_computation.3 | async-start | bytes 2359296 | tf_op jit(solution)/shard_map/reduce_scatter | solution.py:82
  8.7 15.6 %collective-permute-start = (bf16[4,128,768]{1,2,0:T(8,128)(2,1)S(1)}, bf16[4,128,768]{1,2,0:T(8,128)(2,1)S(1)}, u32[]{:S(2)}, u32[]{:S(2)}) collective-permute-start(bf16[4,128,768]{1,2,0:T(8,128)(2,1)S(1)} %copy.11), channel_id=1, source_target_pairs={{0,2},{2,4},{4,6},{6,8},{8,10},{10,12},{12,14},{14,16},{16,18},{18... | collective-permute-start | bytes 2359304 | tf_op jit(solution)/shard_map/ppermute | solution.py:15
  13.8 42.6 %collective-permute-start.2 = (bf16[4,128,768]{1,2,0:T(8,128)(2,1)S(1)}, bf16[4,128,768]{1,2,0:T(8,128)(2,1)S(1)}, u32[]{:S(2)}, u32[]{:S(2)}) collective-permute-start(bf16[4,128,768]{1,2,0:T(8,128)(2,1)S(1)} %copy.11), channel_id=1, source_target_pairs={{2,0},{4,2},{6,4},{8,6},{10,8},{12,10},{14,12},{16,14},{18,16},{20... | collective-permute-start | bytes 2359304 | tf_op jit(solution)/shard_map/ppermute | solution.py:15
  24.3 38.1 %collective-permute-start.1 = (bf16[4,128,768]{1,2,0:T(8,128)(2,1)S(1)}, bf16[4,128,768]{1,2,0:T(8,128)(2,1)}, u32[]{:S(2)}, u32[]{:S(2)}) collective-permute-start(bf16[4,128,768]{1,2,0:T(8,128)(2,1)S(1)} %collective-permute-done), channel_id=1, source_target_pairs={{0,2},{2,4},{4,6},{6,8},{8,10},{10,12},{12,14},{14,16},{16,18},{18... | collective-permute-start | bytes 2359304 | tf_op jit(solution)/shard_map/ppermute | solution.py:15
  56.4 42.1 %collective-permute-start.3 = (bf16[4,128,768]{1,2,0:T(8,128)(2,1)S(1)}, bf16[4,128,768]{1,2,0:T(8,128)(2,1)S(1)}, u32[]{:S(2)}, u32[]{:S(2)}) collective-permute-start(bf16[4,128,768]{1,2,0:T(8,128)(2,1)S(1)} %collective-permute-done.2), channel_id=1, source_target_pairs={{2,0},{4,2},{6,4},{8,6},{10,8},{12,10},{14,12},{16,14},{18,16},{20... | collective-permute-start | bytes 2359304 | tf_op jit(solution)/shard_map/ppermute | solution.py:15
  108.7 1.5 copy-start
  108.7 1.8 copy-start.1
  108.7 2.1 %copy-start.2 = (bf16[640,6,128]{2,0,1:T(8,128)(2,1)S(1)}, bf16[640,6,128]{2,0,1:T(8,128)(2,1)}, u32[]{:S(2)}) copy-start(bf16[640,6,128]{2,0,1:T(8,128)(2,1)} %copy.22) | copy-start | bytes 2949124
  108.7 2.1 %copy-start.3 = (bf16[128,6,128]{2,0,1:T(8,128)(2,1)S(1)}, bf16[128,6,128]{2,0,1:T(8,128)(2,1)}, u32[]{:S(2)}) copy-start(bf16[128,6,128]{2,0,1:T(8,128)(2,1)} %copy.20) | copy-start | bytes 589828
  108.7 2.1 %copy-start.4 = (bf16[128,6,128]{2,0,1:T(8,128)(2,1)S(1)}, bf16[128,6,128]{2,0,1:T(8,128)(2,1)}, u32[]{:S(2)}) copy-start(bf16[128,6,128]{2,0,1:T(8,128)(2,1)} %copy.19) | copy-start | bytes 589828
  109.1 3.1 %slice-start = ((s8[4718592]{0:T(1024)(128)(4,1)}), s8[4194304]{0:T(1024)(128)(4,1)S(1)}, s32[]{:S(2)}) async-start(s8[4718592]{0:T(1024)(128)(4,1)} %bitcast.42), calls=%async_computation.4 | async-start | bytes 8388608
  110.8 1.5 slice-start.1
  114.3 77.8 %reduce-scatter.3.cloned.1.call-start = ((), (), s32[]{:S(2)}) async-start(), calls=%async_computation.2 | async-start | bytes 2359296 | tf_op jit(solution)/shard_map/reduce_scatter | solution.py:81
Sparse Core Ops, SparseCore 0:
  114.5 37.3 reduce-scatter.4
  154.9 37.2 reduce-scatter.2
where the time goes:
time: 201 us
  waiting for transfers between devices  135 us (67%)
  starting transfers between devices  19.7 us (10%)
  local copies, waits for them, and re-layouts  14.6 us (7%)
  between operations  14.2 us (7%)
  matrix products  11.6 us (6%)
  other arithmetic  5.55 us (3%)
    ppermute x4, waiting for transfers between devices, from_behind(): return lax.ppermute(shard, axis, pairs)  63.6 us
    reduce_scatter x1, waiting for transfers between devices, per_device(): lax.psum_scatter(projected, 'head', scatter_dimension=1, tiled=True)  38.4 us
    reduce_scatter x1, waiting for transfers between devices, per_device(): lax.psum_scatter(projected_tan, 'head', scatter_dimension=1, tiled=True)  33.1 us
    ppermute x4, starting transfers between devices, from_behind(): return lax.ppermute(shard, axis, pairs)  19.7 us
    unnamed x21, local copies, waits for them, and re-layouts  6.22 us
    dot_general x1, matrix products, attend(): projected = jnp.dot(att_flat, w_out, preferred_element_type=jnp.float32)  4.3 us
  transfers between devices with their start and end apart: 6, of which 5 were waited for; matrix products, arithmetic and copies ran while one was open for 6% of the time, Pallas kernels for 0%

commit v1 on v0

v1 whole, which is shorter than its diff:
```python
import functools
import math

import jax
import jax.numpy as jnp
from jax import lax
from jax.experimental import pallas as pl
from jax.experimental.pallas import tpu as pltpu
from jax.sharding import PartitionSpec as P

HD = 128
TOK = 128
ROW = 4
WIN = 5 * TOK
SCALE = 1.0 / math.sqrt(HD)
NT = (((1,), (1,)), ((), ()))


def prep_kernel(info, kv, q, send, q_send, q_own):
    for d in range(ROW):
        for t in range(4):
            send[d, t] = kv[t, :, d * HD : (d + 1) * HD]
            s = 4 + d % 2
            send[d, 4 + t] = kv[t, :, s * HD : (s + 1) * HD]
        for t in range(2):
            send[d, 8 + t] = q[t, :, d * HD : (d + 1) * HD]
    odd = info[0] % 2

    @pl.when(odd == 0)
    def _():
        q_own[...] = q[:, :, 4 * HD : 5 * HD]
        q_send[...] = q[:, :, 5 * HD : 6 * HD]

    @pl.when(odd == 1)
    def _():
        q_own[...] = q[:, :, 5 * HD : 6 * HD]
        q_send[...] = q[:, :, 4 * HD : 5 * HD]


def unit(qn, qt, k, v, kt, vt, first_tile, tiles):
    s = lax.dot_general(qn, k, NT, preferred_element_type=jnp.float32) * SCALE
    tile = first_tile + lax.broadcasted_iota(jnp.int32, (1, WIN), 1) // TOK
    s = jnp.where((tile >= 0) & (tile < tiles), s, -jnp.inf)
    e = jnp.exp(s - jnp.max(s, axis=-1, keepdims=True))
    p = e * (1.0 / jnp.sum(e, axis=-1, keepdims=True))
    t = SCALE * lax.dot_general(
        jnp.concatenate([qt, qn], axis=1),
        jnp.concatenate([k, kt], axis=1),
        NT,
        preferred_element_type=jnp.float32,
    )
    w = p * t
    shift = jnp.sum(w, axis=-1, keepdims=True)
    pb = p.astype(jnp.bfloat16)
    wb = w.astype(jnp.bfloat16)
    att = jnp.dot(pb, v, preferred_element_type=jnp.float32)
    tan = (
        jnp.dot(wb, v, preferred_element_type=jnp.float32)
        + jnp.dot(pb, vt, preferred_element_type=jnp.float32)
        - shift * att
    )
    return att.astype(jnp.bfloat16), tan.astype(jnp.bfloat16)


def attend_kernel(tiles, info, r, ha, hb, q_own, q_recv, o_full, o_own, o_other, kf, ks):
    place = info[0]
    q = place % ROW
    row_start = place - q
    odd = q % 2
    low = q < 2
    for t in range(4):
        for j in range(ROW):
            kf[t, (2 + j) * TOK : (3 + j) * TOK, :] = r[j, t]

    @pl.when(low)
    def _():
        for t in range(4):
            for j in range(2):
                kf[t, j * TOK : (j + 1) * TOK, :] = ha[j, t]
                kf[t, (6 + j) * TOK : (7 + j) * TOK, :] = hb[j, t]
                ks[t, j * TOK : (j + 1) * TOK, :] = ha[j, 4 + t]
            for j in range(ROW):
                ks[t, (2 + j) * TOK : (3 + j) * TOK, :] = r[j, 4 + t]

    @pl.when(jnp.logical_not(low))
    def _():
        for t in range(4):
            for j in range(2):
                kf[t, j * TOK : (j + 1) * TOK, :] = hb[j, t]
                kf[t, (6 + j) * TOK : (7 + j) * TOK, :] = ha[j, t]
                ks[t, (4 + j) * TOK : (5 + j) * TOK, :] = ha[j, 4 + t]
            for j in range(ROW):
                ks[t, j * TOK : (j + 1) * TOK, :] = r[j, 4 + t]

    for j in range(ROW):
        at = slice(j * TOK, j * TOK + WIN)
        a, b = unit(
            r[j, 8], r[j, 9], kf[0, at, :], kf[1, at, :], kf[2, at, :], kf[3, at, :],
            row_start + j - 2, tiles,
        )
        o_full[j, 0] = a
        o_full[j, 1] = b
    base = row_start + jnp.where(low, -2, 0)
    for u, qq, out in ((odd, q_own, o_own), (1 - odd, q_recv, o_other)):
        at = pl.ds(pl.multiple_of(u * TOK, TOK), WIN)
        a, b = unit(
            qq[0], qq[1], ks[0, at, :], ks[1, at, :], ks[2, at, :], ks[3, at, :],
            base + u, tiles,
        )
        out[0] = a
        out[1] = b


def far_kernel(info, g, own, recv, w, part, lhs, a):
    @pl.when(pl.program_id(0) == 0)
    def _():
        odd = info[0] % 2
        for t in range(2):
            for h in range(4):
                a[t * TOK : (t + 1) * TOK, h * HD : (h + 1) * HD] = g[h, t]

        @pl.when(odd == 0)
        def _():
            for t in range(2):
                a[t * TOK : (t + 1) * TOK, 4 * HD : 5 * HD] = own[t]
                a[t * TOK : (t + 1) * TOK, 5 * HD : 6 * HD] = recv[t]

        @pl.when(odd == 1)
        def _():
            for t in range(2):
                a[t * TOK : (t + 1) * TOK, 4 * HD : 5 * HD] = recv[t]
                a[t * TOK : (t + 1) * TOK, 5 * HD : 6 * HD] = own[t]

        lhs[...] = a[...]

    part[...] = jnp.dot(a[...], w[...], preferred_element_type=jnp.float32).astype(part.dtype)


def near_kernel(info, lhs, w, part):
    part[...] = jnp.dot(lhs[...], w[...], preferred_element_type=jnp.float32)


def vmem():
    return pl.BlockSpec(memory_space=pltpu.VMEM)


def per_device(queries, keyvals, w_out):
    bf16 = jnp.bfloat16
    ctx_count = lax.axis_size("ctx")
    rows = ctx_count // ROW
    place = lax.axis_index("ctx").astype(jnp.int32)
    side = lax.axis_index("head").astype(jnp.int32)
    info = jnp.stack([place, side])
    low = place % ROW < 2
    smem = pl.BlockSpec(memory_space=pltpu.SMEM)

    send, q_send, q_own = pl.pallas_call(
        prep_kernel,
        in_specs=[smem, vmem(), vmem()],
        out_specs=[vmem()] * 3,
        out_shape=[
            jax.ShapeDtypeStruct((ROW, 10, TOK, HD), bf16),
            jax.ShapeDtypeStruct((2, TOK, HD), bf16),
            jax.ShapeDtypeStruct((2, TOK, HD), bf16),
        ],
        name="prep",
    )(info, keyvals, queries)

    swap = [(i, i ^ 1) for i in range(ctx_count)]
    q_recv = lax.ppermute(q_send, "ctx", swap)
    groups = [[z * ROW + j for j in range(ROW)] for z in range(rows)]
    r = lax.all_to_all(send, "ctx", 0, 0, axis_index_groups=groups, tiled=True)

    up = {i: i + ROW for i in range(ctx_count - ROW)}
    down = {i: i - ROW for i in range(ROW, ctx_count)}
    near_pairs = [(i, d) for i, d in up.items() if i % ROW < 2]
    near_pairs += [(i, d) for i, d in down.items() if i % ROW >= 2]
    far_pairs = [(i, d) for i, d in down.items() if i % ROW < 2]
    far_pairs += [(i, d) for i, d in up.items() if i % ROW >= 2]
    zero = jnp.int32(0)
    two = jnp.int32(2)
    ha = lax.dynamic_slice(r, (jnp.where(low, two, zero), zero, zero, zero), (2, 8, TOK, HD))
    hb = lax.dynamic_slice(r, (jnp.where(low, zero, two), zero, zero, zero), (2, 4, TOK, HD))
    ha = lax.ppermute(ha, "ctx", near_pairs)
    hb = lax.ppermute(hb, "ctx", far_pairs)

    o_full, o_own, o_other = pl.pallas_call(
        functools.partial(attend_kernel, ctx_count),
        in_specs=[smem] + [vmem()] * 5,
        out_specs=[vmem()] * 3,
        out_shape=[
            jax.ShapeDtypeStruct((ROW, 2, TOK, HD), bf16),
            jax.ShapeDtypeStruct((2, TOK, HD), bf16),
            jax.ShapeDtypeStruct((2, TOK, HD), bf16),
        ],
        scratch_shapes=[
            pltpu.VMEM((4, 8 * TOK, HD), bf16),
            pltpu.VMEM((4, 6 * TOK, HD), bf16),
        ],
        cost_estimate=pl.CostEstimate(flops=800_000_000, bytes_accessed=3_000_000, transcendentals=500_000),
        name="attend",
    )(info, r, ha, hb, q_own, q_recv)

    o_recv = lax.ppermute(o_other, "ctx", swap)
    g = lax.all_to_all(o_full, "ctx", 0, 0, axis_index_groups=groups, tiled=True)

    depth, width = w_out.shape
    half = width // 2
    block = half // 3
    far, lhs = pl.pallas_call(
        far_kernel,
        grid_spec=pltpu.PrefetchScalarGridSpec(
            num_scalar_prefetch=1,
            grid=(3,),
            in_specs=[
                pl.BlockSpec((4, 2, TOK, HD), lambda j, s: (0, 0, 0, 0)),
                pl.BlockSpec((2, TOK, HD), lambda j, s: (0, 0, 0)),
                pl.BlockSpec((2, TOK, HD), lambda j, s: (0, 0, 0)),
                pl.BlockSpec((depth, block), lambda j, s: (0, (1 - s[1]) * 3 + j)),
            ],
            out_specs=[
                pl.BlockSpec((2 * TOK, block), lambda j, s: (0, j)),
                pl.BlockSpec((2 * TOK, depth), lambda j, s: (0, 0)),
            ],
            scratch_shapes=[pltpu.VMEM((2 * TOK, depth), bf16)],
        ),
        out_shape=[
            jax.ShapeDtypeStruct((2 * TOK, half), bf16),
            jax.ShapeDtypeStruct((2 * TOK, depth), bf16),
        ],
        cost_estimate=pl.CostEstimate(flops=600_000_000, bytes_accessed=4_000_000, transcendentals=0),
        name="far",
    )(info, g, o_own, o_recv, w_out)
    far = lax.ppermute(far, "head", [(0, 1), (1, 0)])
    near = pl.pallas_call(
        near_kernel,
        grid_spec=pltpu.PrefetchScalarGridSpec(
            num_scalar_prefetch=1,
            grid=(3,),
            in_specs=[
                pl.BlockSpec((2 * TOK, depth), lambda j, s: (0, 0)),
                pl.BlockSpec((depth, block), lambda j, s: (0, s[1] * 3 + j)),
            ],
            out_specs=pl.BlockSpec((2 * TOK, block), lambda j, s: (0, j)),
        ),
        out_shape=jax.ShapeDtypeStruct((2 * TOK, half), jnp.float32),
        cost_estimate=pl.CostEstimate(flops=600_000_000, bytes_accessed=4_000_000, transcendentals=0),
        name="near",
    )(info, lhs, w_out)
    total = (near + far.astype(jnp.float32)).astype(bf16)
    return (total[:TOK], total[TOK:])


def solution(mesh):
    in_specs = (
        P(None, ("batch", "ctx"), "head"),
        P(None, ("batch", "ctx"), "head"),
        P("head", None),
    )
    out_specs = (P(("batch", "ctx"), "head"), P(("batch", "ctx"), "head"))
    return jax.shard_map(
        per_device, mesh=mesh, in_specs=in_specs, out_specs=out_specs, check_vma=False
    )
```

time: 201 us -> 109 us (0.54)
  the two profiles are of different devices: /device:TPU:1 before, /device:TPU:198 now
where the time goes in v1:
time: 109 us; the launch traced here: 108 us
  waiting for transfers between devices  55.3 us (51%)
  starting transfers between devices  29.3 us (27%)
  Pallas kernels  17.8 us (16%)
  local copies, waits for them, and re-layouts  2.56 us (2%)
  other arithmetic  2.24 us (2%)
    all_to_all x1, waiting for transfers between devices, per_device(): r = lax.all_to_all(send, 'ctx', 0, 0, axis_index_groups=groups, tiled=True)  33.6 us
    ppermute x1, waiting for transfers between devices, per_device(): far = lax.ppermute(far, 'head', [(0, 1), (1, 0)])  11.4 us
    all_to_all x1, starting transfers between devices, per_device(): r = lax.all_to_all(send, 'ctx', 0, 0, axis_index_groups=groups, tiled=True)  7.23 us
    pallas_call x1, Pallas kernels, per_device(): pl.pallas_call(functools.partial(attend_kernel, ctx_count), in_specs=[sme...  5.62 us
    ppermute x1, starting transfers between devices, per_device(): ha = lax.ppermute(ha, 'ctx', near_pairs)  5.49 us
    pallas_call x1, Pallas kernels, per_device(): pl.pallas_call(near_kernel, grid_spec=pltpu.PrefetchScalarGridSpec(num_sc...  4.9 us
    ppermute x1, starting transfers between devices, per_device(): o_recv = lax.ppermute(o_other, 'ctx', swap)  4.82 us
    all_to_all x1, starting transfers between devices, per_device(): lax.all_to_all(o_full, 'ctx', 0, 0, axis_index_groups=groups, tiled=True)  4.71 us
  transfers between devices with their start and end apart: 7, of which 6 were waited for; matrix products, arithmetic and copies ran while one was open for 0% of the time, Pallas kernels for 5%

profile of v1, /device:TPU:198, one launch (start us, length us, event | category | flops | bytes accessed | tf_op | source)
XLA Modules:
  0.0 107.9 jit_solution(18068087001043036420)
XLA Ops:
  0.6 0.7 pad_add_fusion.info
  1.3 2.6 %prep.1 = (bf16[4,10,128,128]{3,2,1,0:T(8,128)(2,1)}, bf16[2,128,128]{2,1,0:T(8,128)(2,1)}, bf16[2,128,128]{2,1,0:T(8,128)(2,1)}) custom-call(s32[2]{0:T(128)} %pad_add_fusion.info, bf16[4,128,768]{2,1,0:T(8,128)(2,1)} %kv.1, bf16[2,128,768]{2,1,0:T(8,128)(2,1)} %q.1), custom_call_target="tpu_custom_call" | custom-call | tf_op jit(solution)/shard_map/prep/pallas_call | solution.py:157
  3.9 7.2 %all-to-all-start = ((bf16[4,10,128,128]{3,2,1,0:T(8,128)(2,1)}), bf16[4,10,128,128]{3,2,1,0:T(8,128)(2,1)S(1)}, u32[]{:S(2)}, u32[]{:S(2)}) async-start(bf16[4,10,128,128]{3,2,1,0:T(8,128)(2,1)} %get-tuple-element.10), calls=%async_computation | async-start | bytes 2621440 | tf_op jit(solution)/shard_map/all_to_all | solution.py:172
  11.1 33.6 %all-to-all-done.r = bf16[4,10,128,128]{3,2,1,0:T(8,128)(2,1)S(1)} async-done(((bf16[4,10,128,128]{3,2,1,0:T(8,128)(2,1)}), bf16[4,10,128,128]{3,2,1,0:T(8,128)(2,1)S(1)}, u32[]{:S(2)}, u32[]{:S(2)}) %all-to-all-start) | async-done | bytes 1310752 | tf_op jit(solution)/shard_map/all_to_all | solution.py:172
  44.8 5.5 %collective-permute-start = (bf16[2,8,128,128]{3,2,1,0:T(8,128)(2,1)S(1)}, bf16[2,8,128,128]{3,2,1,0:T(8,128)(2,1)S(1)}, u32[]{:S(2)}, u32[]{:S(2)}) collective-permute-start(bf16[2,8,128,128]{3,2,1,0:T(8,128)(2,1)S(1)} %constant_dynamic-slice_fusion.1), channel_id=1, source_target_pairs={{0,8},{2,10},{8,16},{10,18},{16,24},{18,26},{24,32},{26,34},{32,40... | collective-permute-start | bytes 1572872 | tf_op jit(solution)/shard_map/ppermute | solution.py:184
  50.3 1.9 %collective-permute-start.1 = (bf16[2,4,128,128]{3,2,1,0:T(8,128)(2,1)S(1)}, bf16[2,4,128,128]{3,2,1,0:T(8,128)(2,1)S(1)}, u32[]{:S(2)}, u32[]{:S(2)}) collective-permute-start(bf16[2,4,128,128]{3,2,1,0:T(8,128)(2,1)S(1)} %constant_dynamic-slice_fusion), channel_id=1, source_target_pairs={{8,0},{10,2},{16,8},{18,10},{24,16},{26,18},{32,24},{34,26},{40,32... | collective-permute-start | bytes 786440 | tf_op jit(solution)/shard_map/ppermute | solution.py:185
  52.3 3.2 %collective-permute-start.2 = (bf16[2,128,128]{2,1,0:T(8,128)(2,1)S(1)}, bf16[2,128,128]{2,1,0:T(8,128)(2,1)S(1)}, u32[]{:S(2)}, u32[]{:S(2)}) collective-permute-start(bf16[2,128,128]{2,1,0:T(8,128)(2,1)S(1)} %copy-done.5), channel_id=1, source_target_pairs={{0,2},{2,0},{4,6},{6,4},{8,10},{10,8},{12,14},{14,12},{16,18},{18,... | collective-permute-start | bytes 196616 | tf_op jit(solution)/shard_map/ppermute | solution.py:170
  55.5 3.8 %collective-permute-done.2.q_recv = bf16[2,128,128]{2,1,0:T(8,128)(2,1)S(1)} collective-permute-done((bf16[2,128,128]{2,1,0:T(8,128)(2,1)S(1)}, bf16[2,128,128]{2,1,0:T(8,128)(2,1)S(1)}, u32[]{:S(2)}, u32[]{:S(2)}) %collective-permute-start.2) | collective-permute-done | bytes 65568 | tf_op jit(solution)/shard_map/ppermute | solution.py:170
  59.3 0.5 collective-permute-done.1.hb
  59.8 0.1 copy-done.6
  59.9 0.6 copy-done.4
  60.5 0.2 copy-done.3
  60.7 5.6 %attend.1 = (bf16[4,2,128,128]{3,2,1,0:T(8,128)(2,1)}, bf16[2,128,128]{2,1,0:T(8,128)(2,1)}, bf16[2,128,128]{2,1,0:T(8,128)(2,1)}) custom-call(s32[2]{0:T(128)} %pad_add_fusion.info, bf16[4,10,128,128]{3,2,1,0:T(8,128)(2,1)} %copy-done, bf16[2,8,128,128]{3,2,1,0:T(8,128)(2,1)} %copy-done.3, bf16[2,4,128,128]{3,2,1,0:T(8,128)(2,1)} %copy-done.4, ...), custom_call_target="tpu_custom_call" | custom-call | flops 800000000 | bytes 3000000 | tf_op jit(solution)/shard_map/attend/pallas_call | solution.py:187
  66.3 4.7 %all-to-all-start.1 = ((bf16[4,2,128,128]{3,2,1,0:T(8,128)(2,1)}), bf16[4,2,128,128]{3,2,1,0:T(8,128)(2,1)S(1)}, u32[]{:S(2)}, u32[]{:S(2)}) async-start(bf16[4,2,128,128]{3,2,1,0:T(8,128)(2,1)} %get-tuple-element.13), calls=%async_computation.1 | async-start | bytes 524288 | tf_op jit(solution)/shard_map/all_to_all | solution.py:205
  71.0 4.8 %collective-permute-start.3 = (bf16[2,128,128]{2,1,0:T(8,128)(2,1)}, bf16[2,128,128]{2,1,0:T(8,128)(2,1)S(1)}, u32[]{:S(2)}, u32[]{:S(2)}) collective-permute-start(bf16[2,128,128]{2,1,0:T(8,128)(2,1)} %get-tuple-element.15), channel_id=1, source_target_pairs={{0,2},{2,0},{4,6},{6,4},{8,10},{10,8},{12,14},{14,12},{16,18},{18,... | collective-permute-start | bytes 196616 | tf_op jit(solution)/shard_map/ppermute | solution.py:204
  75.8 3.3 %collective-permute-done.3.recv = bf16[2,128,128]{2,1,0:T(8,128)(2,1)S(1)} collective-permute-done((bf16[2,128,128]{2,1,0:T(8,128)(2,1)}, bf16[2,128,128]{2,1,0:T(8,128)(2,1)S(1)}, u32[]{:S(2)}, u32[]{:S(2)}) %collective-permute-start.3) | collective-permute-done | bytes 65568 | tf_op jit(solution)/shard_map/ppermute | solution.py:204
  79.2 2.6 %all-to-all-done.1.g = bf16[4,2,128,128]{3,2,1,0:T(8,128)(2,1)S(1)} async-done(((bf16[4,2,128,128]{3,2,1,0:T(8,128)(2,1)}), bf16[4,2,128,128]{3,2,1,0:T(8,128)(2,1)S(1)}, u32[]{:S(2)}, u32[]{:S(2)}) %all-to-all-start.1) | async-done | bytes 262176 | tf_op jit(solution)/shard_map/all_to_all | solution.py:205
  81.8 0.7 copy-done.1
  82.5 4.7 %far.1 = (bf16[256,1536]{1,0:T(8,128)(2,1)}, bf16[256,768]{1,0:T(8,128)(2,1)}) custom-call(s32[2]{0:T(128)} %pad_add_fusion.info, bf16[4,2,128,128]{3,2,1,0:T(8,128)(2,1)} %copy-done.1, bf16[2,128,128]{2,1,0:T(8,128)(2,1)} %get-tuple-element.14.own, bf16[2,128,128]{2,1,0:T(8,128)(2,1)} %copy-done.2, bf16[768,3072]{1,0:T(8,128)(2,1)} %w.3), custom_call_target="tpu_custom_call" | custom-call | flops 600000000 | bytes 4000000 | tf_op jit(solution)/shard_map/far/pallas_call | solution.py:210
  87.2 1.9 %collective-permute-start.4 = (bf16[256,1536]{1,0:T(8,128)(2,1)}, bf16[256,1536]{1,0:T(8,128)(2,1)S(1)}, u32[]{:S(2)}, u32[]{:S(2)}) collective-permute-start(bf16[256,1536]{1,0:T(8,128)(2,1)} %get-tuple-element.17), channel_id=1, source_target_pairs={{0,1},{1,0},{2,3},{3,2},{4,5},{5,4},{6,7},{7,6},{8,9},{9,8},{10,11... | collective-permute-start | bytes 2359304 | tf_op jit(solution)/shard_map/ppermute | solution.py:234
  89.1 4.9 %near.1 = f32[256,1536]{1,0:T(8,128)} custom-call(s32[2]{0:T(128)} %pad_add_fusion.info, bf16[256,768]{1,0:T(8,128)(2,1)} %get-tuple-element.16.lhs, bf16[768,3072]{1,0:T(8,128)(2,1)} %w.3), custom_call_target="tpu_custom_call" | custom-call | flops 600000000 | bytes 4000000 | tf_op jit(solution)/shard_map/near/pallas_call | solution.py:235
  94.0 11.4 %collective-permute-done.4 = bf16[256,1536]{1,0:T(8,128)(2,1)S(1)} collective-permute-done((bf16[256,1536]{1,0:T(8,128)(2,1)}, bf16[256,1536]{1,0:T(8,128)(2,1)S(1)}, u32[]{:S(2)}, u32[]{:S(2)}) %collective-permute-start.4) | collective-permute-done | bytes 786464 | tf_op jit(solution)/shard_map/ppermute | solution.py:234
  105.4 1.6 %add_convert_fusion = bf16[256,1536]{1,0:T(8,128)(2,1)S(1)} fusion(f32[256,1536]{1,0:T(8,128)} %near.1, bf16[256,1536]{1,0:T(8,128)(2,1)S(1)} %collective-permute-done.4), kind=kLoop, calls=%fused_computation | loop fusion | flops 1179648 | bytes 3145728 | tf_op jit(solution)/shard_map/convert_element_type | solution.py:250
  107.0 0.9 fusion
  (13 shorter events, 0.1 us)
Async XLA Ops:
  3.9 48.4 %copy-start.5 = (bf16[2,128,128]{2,1,0:T(8,128)(2,1)S(1)}, bf16[2,128,128]{2,1,0:T(8,128)(2,1)}, u32[]{:S(2)}) copy-start(bf16[2,128,128]{2,1,0:T(8,128)(2,1)} %get-tuple-element.12) | copy-start | bytes 196612
  3.9 40.8 %all-to-all-start = ((bf16[4,10,128,128]{3,2,1,0:T(8,128)(2,1)}), bf16[4,10,128,128]{3,2,1,0:T(8,128)(2,1)S(1)}, u32[]{:S(2)}, u32[]{:S(2)}) async-start(bf16[4,10,128,128]{3,2,1,0:T(8,128)(2,1)} %get-tuple-element.10), calls=%async_computation | async-start | bytes 2621440 | tf_op jit(solution)/shard_map/all_to_all | solution.py:172
  44.7 15.1 %copy-start = (bf16[4,10,128,128]{3,2,1,0:T(8,128)(2,1)}, bf16[4,10,128,128]{3,2,1,0:T(8,128)(2,1)S(1)}, u32[]{:S(2)}) copy-start(bf16[4,10,128,128]{3,2,1,0:T(8,128)(2,1)S(1)} %all-to-all-done.r) | copy-start | bytes 3932164
  44.8 15.0 %collective-permute-start = (bf16[2,8,128,128]{3,2,1,0:T(8,128)(2,1)S(1)}, bf16[2,8,128,128]{3,2,1,0:T(8,128)(2,1)S(1)}, u32[]{:S(2)}, u32[]{:S(2)}) collective-permute-start(bf16[2,8,128,128]{3,2,1,0:T(8,128)(2,1)S(1)} %constant_dynamic-slice_fusion.1), channel_id=1, source_target_pairs={{0,8},{2,10},{8,16},{10,18},{16,24},{18,26},{24,32},{26,34},{32,40... | collective-permute-start | bytes 1572872 | tf_op jit(solution)/shard_map/ppermute | solution.py:184
  50.3 9.5 %collective-permute-start.1 = (bf16[2,4,128,128]{3,2,1,0:T(8,128)(2,1)S(1)}, bf16[2,4,128,128]{3,2,1,0:T(8,128)(2,1)S(1)}, u32[]{:S(2)}, u32[]{:S(2)}) collective-permute-start(bf16[2,4,128,128]{3,2,1,0:T(8,128)(2,1)S(1)} %constant_dynamic-slice_fusion), channel_id=1, source_target_pairs={{8,0},{10,2},{16,8},{18,10},{24,16},{26,18},{32,24},{34,26},{40,32... | collective-permute-start | bytes 786440 | tf_op jit(solution)/shard_map/ppermute | solution.py:185
  52.3 7.1 %collective-permute-start.2 = (bf16[2,128,128]{2,1,0:T(8,128)(2,1)S(1)}, bf16[2,128,128]{2,1,0:T(8,128)(2,1)S(1)}, u32[]{:S(2)}, u32[]{:S(2)}) collective-permute-start(bf16[2,128,128]{2,1,0:T(8,128)(2,1)S(1)} %copy-done.5), channel_id=1, source_target_pairs={{0,2},{2,0},{4,6},{6,4},{8,10},{10,8},{12,14},{14,12},{16,18},{18,... | collective-permute-start | bytes 196616 | tf_op jit(solution)/shard_map/ppermute | solution.py:170
  59.3 0.6 copy-start.6
  59.8 0.7 copy-start.4
  59.8 0.9 copy-start.3
  66.3 15.5 %all-to-all-start.1 = ((bf16[4,2,128,128]{3,2,1,0:T(8,128)(2,1)}), bf16[4,2,128,128]{3,2,1,0:T(8,128)(2,1)S(1)}, u32[]{:S(2)}, u32[]{:S(2)}) async-start(bf16[4,2,128,128]{3,2,1,0:T(8,128)(2,1)} %get-tuple-element.13), calls=%async_computation.1 | async-start | bytes 524288 | tf_op jit(solution)/shard_map/all_to_all | solution.py:205
  71.0 8.1 %collective-permute-start.3 = (bf16[2,128,128]{2,1,0:T(8,128)(2,1)}, bf16[2,128,128]{2,1,0:T(8,128)(2,1)S(1)}, u32[]{:S(2)}, u32[]{:S(2)}) collective-permute-start(bf16[2,128,128]{2,1,0:T(8,128)(2,1)} %get-tuple-element.15), channel_id=1, source_target_pairs={{0,2},{2,0},{4,6},{6,4},{8,10},{10,8},{12,14},{14,12},{16,18},{18,... | collective-permute-start | bytes 196616 | tf_op jit(solution)/shard_map/ppermute | solution.py:204
  79.2 2.6 %copy-start.2 = (bf16[2,128,128]{2,1,0:T(8,128)(2,1)}, bf16[2,128,128]{2,1,0:T(8,128)(2,1)S(1)}, u32[]{:S(2)}) copy-start(bf16[2,128,128]{2,1,0:T(8,128)(2,1)S(1)} %collective-permute-done.3.recv) | copy-start | bytes 196612
  81.8 0.7 copy-start.1
  87.2 18.2 %collective-permute-start.4 = (bf16[256,1536]{1,0:T(8,128)(2,1)}, bf16[256,1536]{1,0:T(8,128)(2,1)S(1)}, u32[]{:S(2)}, u32[]{:S(2)}) collective-permute-start(bf16[256,1536]{1,0:T(8,128)(2,1)} %get-tuple-element.17), channel_id=1, source_target_pairs={{0,1},{1,0},{2,3},{3,2},{4,5},{5,4},{6,7},{7,6},{8,9},{9,8},{10,11... | collective-permute-start | bytes 2359304 | tf_op jit(solution)/shard_map/ppermute | solution.py:234
